TPU v7x, 32 devices: a whole 2x2x4 slice. The times are simulated.
32 devices in a mesh: groups: 2 (over x), ctx: 16 (over z, y, core).
Axes of the slice: x: 2, y: 2, z: 4, core: 2. Of those that a mesh axis runs over, the one named last changes fastest.
Arguments:
- features: bfloat16 [64, 16, 24, 192], P(('groups', 'ctx')), parts along dimension 0, may hold values from -6 to 6
- clip_ids: int32 [64], P('groups'), parts along dimension 0, may hold values from 0 to 7, never falling along the last dimension, each value on 1 to 8 neighbouring positions
- gain_first: float32 [192], replicated, may hold values from 0.1 to 1.9
- weight_first: bfloat16 [27, 192, 192], P(None, None, 'ctx'), may hold values from -0.078125 to 0.078125
- gain_second: float32 [192], replicated, may hold values from 0.1 to 1.9
- weight_second: bfloat16 [27, 192, 192], P(None, None, 'ctx'), may hold values from -0.078125 to 0.078125
- gain_third: float32 [192], replicated, may hold values from 0.1 to 1.9
- weight_out: bfloat16 [27, 192, 16], replicated, may hold values from -0.078125 to 0.078125
- embed_weight: bfloat16 [64, 3072], replicated, may hold values from -0.75 to 0.75
- shift_mod: float32 [3072], replicated, may hold values from -3 to 3
- scale_mod: float32 [3072], replicated, may hold values from -0.5 to 0.5
- token_order: int32 [6144], P(('groups', 'ctx')), parts along dimension 0, may hold values from 0 to 3071, each once
Outputs:
- tokens_out: bfloat16 [6144, 3072], P(('groups', 'ctx')), parts along dimension 0
There are 2 independent parts, one for each index of `groups`. A program takes and returns all parts, laid end to end along the dimension named above; an argument that names none is the same for every part. Nothing has to cross between parts.
Inputs may be any that keep to these rules, and one draw needn't show every extreme that they name: `clip_ids`: clip ids never fall along the frames and start at 0; each clip spans 1 to 8 frames, and some clip spans exactly 8. `token_order`: each patch index appears exactly once.
All inputs are finite; a program needn't handle non-finite values.
Results may differ from a plain program's by a relative error of at most 0.014.
Values may be sent and summed in bfloat16 or wider, within the bound.
A program may use at most 128 MiB of HBM per device.

v0:
```python
import jax
import jax.numpy as jnp
from jax import lax
from jax.sharding import PartitionSpec as P


def shifted_2(value, axis, steps):
    count = lax.axis_size(axis)
    first, last = (max(0, -steps), min(count, count - steps))
    return lax.ppermute(value, axis, [(source, source + steps) for source in range(first, last)])


def clip_masks(clip_ids, device, frames):
    positions = device * frames - 2 + jnp.arange(frames + 2, dtype=jnp.int32)
    looked = jnp.where(positions >= 0, clip_ids[jnp.maximum(positions, 0)], -1)
    current = looked[2:]
    return jnp.stack([looked[frame_tap : frame_tap + frames] == current for frame_tap in range(3)])


def conv_block(extended, kept_mask, weight):
    frames = kept_mask.shape[1]
    height, breadth, channels = (extended.shape[1], extended.shape[2], extended.shape[3])
    padded = jnp.pad(extended, ((0, 0), (1, 1), (1, 1), (0, 0)))
    summed = jnp.zeros((frames * height * breadth, weight.shape[2]), jnp.float32)
    for frame_tap in range(3):
        source = jnp.where(
            kept_mask[frame_tap][:, None, None, None],
            padded[frame_tap : frame_tap + frames],
            jnp.zeros((), extended.dtype),
        )
        for row_tap in range(3):
            for col_tap in range(3):
                shifted = source[
                    :, row_tap : row_tap + height, col_tap : col_tap + breadth, :
                ].reshape(-1, channels)
                summed = summed + jnp.dot(
                    shifted,
                    weight[frame_tap * 9 + row_tap * 3 + col_tap],
                    preferred_element_type=jnp.float32,
                )
    return summed


def with_rim(values):
    rim = shifted_2(values, "ctx", 1)
    return jnp.concatenate([rim, values], axis=0)


def conv_columns(extended, kept_mask, weight_shard):
    return conv_block(extended, kept_mask, lax.all_gather(weight_shard, "ctx", axis=2, tiled=True))


def rms_silu(values, gain_vector):
    values = values.astype(jnp.float32)
    normed = (
        values * lax.rsqrt(jnp.mean(values * values, axis=-1, keepdims=True) + 1e-06) * gain_vector
    )
    return jax.nn.silu(normed).astype(jnp.bfloat16)


def to_patches(latents):
    frames, height, breadth, latent_depth = latents.shape
    grid = latents.reshape(frames, height // 2, 2, breadth // 2, 2, latent_depth).transpose(
        0, 1, 3, 2, 4, 5
    )
    return grid.reshape(frames * (height // 2) * (breadth // 2), 4 * latent_depth)


def modulate(ordered, embed_weight, shift_mod, scale_mod):
    embedded = jnp.dot(ordered, embed_weight, preferred_element_type=jnp.float32)
    center = jnp.mean(embedded, axis=-1, keepdims=True)
    centered = embedded - center
    variance = jnp.mean(centered * centered, axis=-1, keepdims=True)
    normed = centered * lax.rsqrt(variance + 1e-06)
    return (normed * (1.0 + scale_mod) + shift_mod).astype(jnp.bfloat16)


def body(
    features,
    clip_ids,
    gain_first,
    weight_first,
    gain_second,
    weight_second,
    gain_third,
    weight_out,
    embed_weight,
    shift_mod,
    scale_mod,
    token_order,
):
    frames, height, breadth, channels = features.shape
    kept_mask = clip_masks(clip_ids, lax.axis_index("ctx"), frames)

    def convolve(values, weight_shard):
        extended = with_rim(values)
        summed = conv_columns(extended, kept_mask, weight_shard)
        return summed.reshape(frames, height, breadth, channels)

    first_in = rms_silu(features, gain_first)
    first_out = convolve(first_in, weight_first).astype(jnp.bfloat16)
    second_in = rms_silu(first_out, gain_second)
    block_out = (features.astype(jnp.float32) + convolve(second_in, weight_second)).astype(
        jnp.bfloat16
    )
    head_in = rms_silu(block_out, gain_third)
    latents = (
        conv_block(with_rim(head_in), kept_mask, weight_out)
        .reshape(frames, height, breadth, -1)
        .astype(jnp.bfloat16)
    )
    patches = to_patches(latents)
    all_patches = lax.all_gather(patches, "ctx", axis=0, tiled=True)
    ordered = all_patches[token_order]
    return modulate(ordered, embed_weight, shift_mod, scale_mod)


def solution(mesh):
    in_specs = (
        P(("groups", "ctx"), None, None, None),
        P("groups"),
        P(),
        P(None, None, "ctx"),
        P(),
        P(None, None, "ctx"),
        P(),
        P(),
        P(),
        P(),
        P(),
        P(("groups", "ctx")),
    )
    out_specs = P(("groups", "ctx"), None)
    return jax.shard_map(body, mesh=mesh, in_specs=in_specs, out_specs=out_specs, check_vma=False)
```

profile of v0, /device:TPU:0, one launch (start us, length us, event | category | flops | bytes accessed | tf_op | source)
XLA Modules:
  0.0 207.2 jit_solution(17634757845780341969)
XLA Ops:
  7.3 1.2 fusion.31
  8.5 1.3 fusion.38
  9.8 2.4 %collective-permute-start = (bf16[2,16,24,192]{3,2,1,0:T(8,128)(2,1)S(1)}, bf16[2,16,24,192]{3,2,1,0:T(8,128)(2,1)S(1)}, u32[]{:S(2)}, u32[]{:S(2)}) collective-permute-start(bf16[2,16,24,192]{3,2,1,0:T(8,128)(2,1)S(1)} %fusion.38), channel_id=1, source_target_pairs={{0,1},{1,2},{2,3},{3,4},{4,5},{5,6},{6,7},{7,8},{8,9},{9,10},{10,1... | collective-permute-start | bytes 884744 | tf_op jit(solution)/shard_map/ppermute | solution.py:10
  12.3 1.3 gather_fusion
  13.6 1.2 compare_select_fusion
  16.2 2.1 %fusion.168 = (bf16[2,16,24,192]{3,2,1,0:T(8,128)(2,1)}, bf16[2,16,24,192]{3,2,1,0:T(8,128)(2,1)}, bf16[2,16,24,192]{3,2,1,0:T(8,128)(2,1)}, bf16[2,16,24,192]{3...) fusion(bf16[4,18,26,192]{3,2,1,0:T(8,128)(2,1)S(1)} %fusion.14), kind=kLoop, calls=%fused_computation.275 | loop fusion | bytes 4718592 | tf_op jit(solution)/shard_map/slice | solution.py:33
  18.5 3.3 %fusion.173 = (bf16[2,16,24,192]{3,2,1,0:T(8,128)(2,1)}, bf16[2,16,24,192]{3,2,1,0:T(8,128)(2,1)}, bf16[2,16,24,192]{3,2,1,0:T(8,128)(2,1)}, bf16[2,16,24,192]{3...) fusion(bf16[2,18,26,192]{3,2,1,0:T(8,128)(2,1)S(1)} %get-tuple-, ...), kind=kLoop, calls=%fused_computation.280 | loop fusion | bytes 10616832 | tf_op jit(solution)/shard_map/slice | solution.py:33
  21.8 36.0 %all-gather.4.cloned.1.call-done = bf16[27,192,192]{1,0,2:T(8,128)(2,1)} async-done(((bf16[27,192,12]{1,0,2:T(8,128)(2,1)}), bf16[27,192,192]{1,0,2:T(8,128)(2,1)}) %all-gather.4.cloned.1.call-update) | async-done | bytes 1990672 | tf_op jit(solution)/shard_map/all_gather | solution.py:50
  57.8 7.2 %fusion.165 = (bf16[1,192,192]{1,0,2:T(2,128)(2,1)}, bf16[1,192,192]{1,0,2:T(2,128)(2,1)}, bf16[1,192,192]{1,0,2:T(2,128)(2,1)}, bf16[1,192,192]{1,0,2:T(2,128)(...) fusion(bf16[27,192,192]{1,0,2:T(8,128)(2,1)} %all-gather.4.clon, ...), kind=kLoop, calls=%fused_computation.272 | loop fusion | bytes 1179648 | tf_op jit(solution)/shard_map/slice | solution.py:38
  65.0 1.7 copy.83
  66.7 1.7 copy.84
  68.4 1.7 copy.85
  70.1 1.7 copy.86
  71.7 1.7 copy.87
  73.4 1.7 copy.88
  75.1 1.7 copy.89
  76.8 1.7 copy.90
  78.5 4.9 %fusion.164 = (bf16[1,192,192]{1,0,2:T(2,128)(2,1)}, bf16[1,192,192]{1,0,2:T(2,128)(2,1)}, bf16[1,192,192]{1,0,2:T(2,128)(2,1)}, bf16[1,192,192]{1,0,2:T(2,128)(...) fusion(bf16[27,192,192]{1,0,2:T(8,128)(2,1)S(1)} %copy-done.2), kind=kLoop, calls=%fused_computation.271 | loop fusion | bytes 2801664 | tf_op jit(solution)/shard_map/slice | solution.py:38
  83.4 1.1 copy.91
  84.5 1.0 copy.92
  85.6 1.0 copy.93
  86.6 1.0 copy.94
  87.7 1.1 copy.95
  88.7 1.1 copy.96
  89.8 1.7 copy.97
  91.5 1.3 fusion.97
  99.4 1.7 copy.100
  101.2 0.8 copy.101
  103.2 1.2 convolution_add_fusion.37
  108.9 2.9 %collective-permute-start.1 = (bf16[2,16,24,192]{3,2,1,0:T(8,128)(2,1)S(1)}, bf16[2,16,24,192]{3,2,1,0:T(8,128)(2,1)}, u32[]{:S(2)}, u32[]{:S(2)}) collective-permute-start(bf16[2,16,24,192]{3,2,1,0:T(8,128)(2,1)S(1)} %multiply_convert_fusion), channel_id=1, source_target_pairs={{0,1},{1,2},{2,3},{3,4},{4,5},{5,6},{6,7},{7,8},{8,9},{9,10},{10,1... | collective-permute-start | bytes 884744 | tf_op jit(solution)/shard_map/ppermute | solution.py:10
  111.8 9.6 %fusion.162 = (bf16[1,192,192]{1,0,2:T(2,128)(2,1)S(1)}, bf16[1,192,192]{1,0,2:T(2,128)(2,1)S(1)}, bf16[1,192,192]{1,0,2:T(2,128)(2,1)S(1)}, bf16[1,192,192]{1,0...) fusion(bf16[27,192,192]{1,0,2:T(8,128)(2,1)} %all-gather.6.clon, ...), kind=kLoop, calls=%fused_computation.269 | loop fusion | bytes 2801664 | tf_op jit(solution)/shard_map/slice | solution.py:38
  121.4 1.4 fusion.163
  125.1 0.8 copy.113
  129.0 1.7 copy.118
  130.7 1.7 copy.119
  132.4 1.7 copy.120
  134.1 1.7 copy.121
  135.8 1.7 copy.122
  137.5 1.7 copy.123
  139.1 1.7 copy.124
  140.8 1.7 copy.125
  145.3 1.5 fusion.13
  146.9 0.8 slice_select_fusion.2
  158.8 1.9 collective-permute-start.2
  160.9 0.8 collective-permute-done.2
  171.0 25.7 %all-gather = bf16[16,192,64]{1,2,0:T(8,128)(2,1)S(1)} all-gather(bf16[1,192,64]{1,2,0:T(8,128)(2,1)S(1)} %reshape.421), channel_id=1, replica_groups=mesh['groups'=2,'ctx'=16] {'ctx'}, dimensions={0}, use_global_device_ids=true | all-gather | bytes 417792 | tf_op jit(solution)/shard_map/all_gather | solution.py:113
  197.1 0.8 gather_fusion.1
  198.9 1.5 add_convert_fusion
  (325 shorter events, 43.7 us)
Async XLA Ops:
  6.5 191.4 %copy-start = (bf16[64,3072]{1,0:T(8,128)(2,1)S(1)}, bf16[64,3072]{1,0:T(8,128)(2,1)}, u32[]{:S(2)}) copy-start(bf16[64,3072]{1,0:T(8,128)(2,1)} %param.20) | copy-start | bytes 1179652
  6.5 51.3 %all-gather.4.cloned.1.call-start = ((), (), s32[]{:S(2)}) async-start(), calls=%async_computation | async-start | bytes 3342336 | tf_op jit(solution)/shard_map/all_gather | solution.py:50
  7.3 104.5 %all-gather.6.cloned.1.call-start = ((), (), s32[]{:S(2)}) async-start(), calls=%async_computation.1 | async-start | bytes 3342336 | tf_op jit(solution)/shard_map/all_gather | solution.py:50
  9.8 8.5 %copy-start.4 = (bf16[2,16,24,192]{3,2,1,0:T(8,128)(2,1)}, bf16[2,16,24,192]{3,2,1,0:T(8,128)(2,1)S(1)}, u32[]{:S(2)}) copy-start(bf16[2,16,24,192]{3,2,1,0:T(8,128)(2,1)S(1)} %fusion.38) | copy-start | bytes 884740
  9.8 5.8 %collective-permute-start = (bf16[2,16,24,192]{3,2,1,0:T(8,128)(2,1)S(1)}, bf16[2,16,24,192]{3,2,1,0:T(8,128)(2,1)S(1)}, u32[]{:S(2)}, u32[]{:S(2)}) collective-permute-start(bf16[2,16,24,192]{3,2,1,0:T(8,128)(2,1)S(1)} %fusion.38), channel_id=1, source_target_pairs={{0,1},{1,2},{2,3},{3,4},{4,5},{5,6},{6,7},{7,8},{8,9},{9,10},{10,1... | collective-permute-start | bytes 884744 | tf_op jit(solution)/shard_map/ppermute | solution.py:10
  14.9 3.4 %copy-start.81 = (pred[2]{0:T(512)(128)(4,1)}, pred[2]{0:T(512)(128)(4,1)S(1)}, u32[]{:S(2)}) copy-start(pred[2]{0:T(512)(128)(4,1)S(1)} %get-tuple-element.143) | copy-start | bytes 10
  14.9 3.4 %copy-start.83 = (pred[2]{0:T(512)(128)(4,1)}, pred[2]{0:T(512)(128)(4,1)S(1)}, u32[]{:S(2)}) copy-start(pred[2]{0:T(512)(128)(4,1)S(1)} %get-tuple-element.144) | copy-start | bytes 10
  57.8 20.6 %copy-start.2 = (bf16[27,192,192]{1,0,2:T(8,128)(2,1)S(1)}, bf16[27,192,192]{1,0,2:T(8,128)(2,1)}, u32[]{:S(2)}) copy-start(bf16[27,192,192]{1,0,2:T(8,128)(2,1)} %all-gather.4.cloned.1.call-done) | copy-start | bytes 5971972
  83.4 9.5 %copy-start.22 = (bf16[2,16,24,192]{3,2,1,0:T(8,128)(2,1)S(1)}, bf16[2,16,24,192]{3,2,1,0:T(8,128)(2,1)}, u32[]{:S(2)}) copy-start(bf16[2,16,24,192]{3,2,1,0:T(8,128)(2,1)} %get-tuple-element.150) | copy-start | bytes 884740
  83.4 9.5 %copy-start.75 = (bf16[1,192,192]{2,1,0:T(8,128)(2,1)S(1)}, bf16[1,192,192]{2,1,0:T(8,128)(2,1)}, u32[]{:S(2)}) copy-start(bf16[1,192,192]{2,1,0:T(8,128)(2,1)} %copy.84) | copy-start | bytes 221188
  83.4 9.8 %copy-start.21 = (bf16[2,16,24,192]{3,2,1,0:T(8,128)(2,1)S(1)}, bf16[2,16,24,192]{3,2,1,0:T(8,128)(2,1)}, u32[]{:S(2)}) copy-start(bf16[2,16,24,192]{3,2,1,0:T(8,128)(2,1)} %get-tuple-element.151) | copy-start | bytes 884740
  83.4 9.8 %copy-start.74 = (bf16[1,192,192]{2,1,0:T(8,128)(2,1)S(1)}, bf16[1,192,192]{2,1,0:T(8,128)(2,1)}, u32[]{:S(2)}) copy-start(bf16[1,192,192]{2,1,0:T(8,128)(2,1)} %copy.85) | copy-start | bytes 221188
  89.8 3.8 %copy-start.20 = (bf16[2,16,24,192]{3,2,1,0:T(8,128)(2,1)S(1)}, bf16[2,16,24,192]{3,2,1,0:T(8,128)(2,1)}, u32[]{:S(2)}) copy-start(bf16[2,16,24,192]{3,2,1,0:T(8,128)(2,1)} %get-tuple-element.152) | copy-start | bytes 884740
  89.8 3.8 %copy-start.72 = (bf16[1,192,192]{2,1,0:T(8,128)(2,1)S(1)}, bf16[1,192,192]{2,1,0:T(8,128)(2,1)}, u32[]{:S(2)}) copy-start(bf16[1,192,192]{2,1,0:T(8,128)(2,1)} %copy.86) | copy-start | bytes 221188
  96.8 1.8 copy-start.40
  97.1 4.0 %copy-start.39 = (bf16[1,192,192]{1,0,2:T(2,128)(2,1)S(1)}, bf16[1,192,192]{1,0,2:T(2,128)(2,1)}, u32[]{:S(2)}) copy-start(bf16[1,192,192]{1,0,2:T(2,128)(2,1)} %get-tuple-element.40) | copy-start | bytes 221188
  97.1 4.8 %copy-start.38 = (bf16[1,192,192]{1,0,2:T(2,128)(2,1)S(1)}, bf16[1,192,192]{1,0,2:T(2,128)(2,1)}, u32[]{:S(2)}) copy-start(bf16[1,192,192]{1,0,2:T(2,128)(2,1)} %get-tuple-element.39) | copy-start | bytes 221188
  97.1 4.9 %copy-start.37 = (bf16[1,192,192]{1,0,2:T(2,128)(2,1)S(1)}, bf16[1,192,192]{1,0,2:T(2,128)(2,1)}, u32[]{:S(2)}) copy-start(bf16[1,192,192]{1,0,2:T(2,128)(2,1)} %get-tuple-element.38) | copy-start | bytes 221188
  97.2 5.1 %copy-start.36 = (bf16[1,192,192]{1,0,2:T(2,128)(2,1)S(1)}, bf16[1,192,192]{1,0,2:T(2,128)(2,1)}, u32[]{:S(2)}) copy-start(bf16[1,192,192]{1,0,2:T(2,128)(2,1)} %get-tuple-element.37) | copy-start | bytes 221188
  97.2 5.2 %copy-start.35 = (bf16[1,192,192]{1,0,2:T(2,128)(2,1)S(1)}, bf16[1,192,192]{1,0,2:T(2,128)(2,1)}, u32[]{:S(2)}) copy-start(bf16[1,192,192]{1,0,2:T(2,128)(2,1)} %get-tuple-element.36) | copy-start | bytes 221188
  97.5 5.1 %copy-start.34 = (bf16[1,192,192]{1,0,2:T(2,128)(2,1)S(1)}, bf16[1,192,192]{1,0,2:T(2,128)(2,1)}, u32[]{:S(2)}) copy-start(bf16[1,192,192]{1,0,2:T(2,128)(2,1)} %get-tuple-element.35) | copy-start | bytes 221188
  97.5 5.2 %copy-start.33 = (bf16[1,192,192]{1,0,2:T(2,128)(2,1)S(1)}, bf16[1,192,192]{1,0,2:T(2,128)(2,1)}, u32[]{:S(2)}) copy-start(bf16[1,192,192]{1,0,2:T(2,128)(2,1)} %get-tuple-element.34) | copy-start | bytes 221188
  97.5 5.3 %copy-start.32 = (bf16[1,192,192]{1,0,2:T(2,128)(2,1)S(1)}, bf16[1,192,192]{1,0,2:T(2,128)(2,1)}, u32[]{:S(2)}) copy-start(bf16[1,192,192]{1,0,2:T(2,128)(2,1)} %get-tuple-element.33) | copy-start | bytes 221188
  97.5 5.5 %copy-start.31 = (bf16[1,192,192]{1,0,2:T(2,128)(2,1)S(1)}, bf16[1,192,192]{1,0,2:T(2,128)(2,1)}, u32[]{:S(2)}) copy-start(bf16[1,192,192]{1,0,2:T(2,128)(2,1)} %get-tuple-element.32) | copy-start | bytes 221188
  97.5 5.6 %copy-start.8 = (bf16[2,16,24,192]{3,2,1,0:T(8,128)(2,1)S(1)}, bf16[2,16,24,192]{3,2,1,0:T(8,128)(2,1)}, u32[]{:S(2)}) copy-start(bf16[2,16,24,192]{3,2,1,0:T(8,128)(2,1)} %get-tuple-element.127) | copy-start | bytes 884740
  99.4 5.0 %copy-start.7 = (bf16[2,16,24,192]{3,2,1,0:T(8,128)(2,1)S(1)}, bf16[2,16,24,192]{3,2,1,0:T(8,128)(2,1)}, u32[]{:S(2)}) copy-start(bf16[2,16,24,192]{3,2,1,0:T(8,128)(2,1)} %get-tuple-element.126) | copy-start | bytes 884740
  102.4 2.4 %copy-start.6 = (bf16[2,16,24,192]{3,2,1,0:T(8,128)(2,1)S(1)}, bf16[2,16,24,192]{3,2,1,0:T(8,128)(2,1)}, u32[]{:S(2)}) copy-start(bf16[2,16,24,192]{3,2,1,0:T(8,128)(2,1)} %get-tuple-element.125) | copy-start | bytes 884740
  102.5 2.2 %copy-start.77 = (bf16[1,192,192]{2,1,0:T(8,128)(2,1)S(1)}, bf16[1,192,192]{2,1,0:T(8,128)(2,1)}, u32[]{:S(2)}) copy-start(bf16[1,192,192]{2,1,0:T(8,128)(2,1)} %copy.100) | copy-start | bytes 221188
  102.7 1.7 copy-start.78
  103.2 1.9 copy-start.30
  103.2 1.9 copy-start.76
  108.9 36.4 %collective-permute-start.1 = (bf16[2,16,24,192]{3,2,1,0:T(8,128)(2,1)S(1)}, bf16[2,16,24,192]{3,2,1,0:T(8,128)(2,1)}, u32[]{:S(2)}, u32[]{:S(2)}) collective-permute-start(bf16[2,16,24,192]{3,2,1,0:T(8,128)(2,1)S(1)} %multiply_convert_fusion), channel_id=1, source_target_pairs={{0,1},{1,2},{2,3},{3,4},{4,5},{5,6},{6,7},{7,8},{8,9},{9,10},{10,1... | collective-permute-start | bytes 884744 | tf_op jit(solution)/shard_map/ppermute | solution.py:10
  111.8 9.6 %copy-start.1 = (bf16[27,192,192]{1,0,2:T(8,128)(2,1)S(1)}, bf16[27,192,192]{1,0,2:T(8,128)(2,1)}, u32[]{:S(2)}) copy-start(bf16[27,192,192]{1,0,2:T(8,128)(2,1)} %all-gather.6.cloned.1.call-done) | copy-start | bytes 5971972
  123.6 19.7 %copy-start.48 = (bf16[1,192,192]{1,0,2:T(2,128)(2,1)S(1)}, bf16[1,192,192]{1,0,2:T(2,128)(2,1)}, u32[]{:S(2)}) copy-start(bf16[1,192,192]{1,0,2:T(2,128)(2,1)} %get-tuple-element.14) | copy-start | bytes 221188
  124.4 19.7 %copy-start.47 = (bf16[1,192,192]{1,0,2:T(2,128)(2,1)S(1)}, bf16[1,192,192]{1,0,2:T(2,128)(2,1)}, u32[]{:S(2)}) copy-start(bf16[1,192,192]{1,0,2:T(2,128)(2,1)} %get-tuple-element.13) | copy-start | bytes 221188
  125.1 19.0 %copy-start.46 = (bf16[1,192,192]{1,0,2:T(2,128)(2,1)S(1)}, bf16[1,192,192]{1,0,2:T(2,128)(2,1)}, u32[]{:S(2)}) copy-start(bf16[1,192,192]{1,0,2:T(2,128)(2,1)} %get-tuple-element.12) | copy-start | bytes 221188
  125.9 18.4 %copy-start.45 = (bf16[1,192,192]{1,0,2:T(2,128)(2,1)S(1)}, bf16[1,192,192]{1,0,2:T(2,128)(2,1)}, u32[]{:S(2)}) copy-start(bf16[1,192,192]{1,0,2:T(2,128)(2,1)} %get-tuple-element.11) | copy-start | bytes 221188
  126.7 17.8 %copy-start.44 = (bf16[1,192,192]{1,0,2:T(2,128)(2,1)S(1)}, bf16[1,192,192]{1,0,2:T(2,128)(2,1)}, u32[]{:S(2)}) copy-start(bf16[1,192,192]{1,0,2:T(2,128)(2,1)} %get-tuple-element.10) | copy-start | bytes 221188
  127.5 17.2 %copy-start.43 = (bf16[1,192,192]{1,0,2:T(2,128)(2,1)S(1)}, bf16[1,192,192]{1,0,2:T(2,128)(2,1)}, u32[]{:S(2)}) copy-start(bf16[1,192,192]{1,0,2:T(2,128)(2,1)} %get-tuple-element.9) | copy-start | bytes 221188
  128.2 16.5 %copy-start.42 = (bf16[1,192,192]{1,0,2:T(2,128)(2,1)S(1)}, bf16[1,192,192]{1,0,2:T(2,128)(2,1)}, u32[]{:S(2)}) copy-start(bf16[1,192,192]{1,0,2:T(2,128)(2,1)} %get-tuple-element.8) | copy-start | bytes 221188
  129.0 13.5 %copy-start.49 = (bf16[1,192,192]{1,0,2:T(2,128)(2,1)S(1)}, bf16[1,192,192]{1,0,2:T(2,128)(2,1)}, u32[]{:S(2)}) copy-start(bf16[1,192,192]{1,0,2:T(2,128)(2,1)} %get-tuple-element.15) | copy-start | bytes 221188
  148.3 1.2 copy-start.66
  148.7 1.5 copy-start.64
  157.9 2.8 %copy-start.85 = (s32[192]{0:T(256)S(1)}, s32[192]{0:T(256)}, u32[]{:S(2)}) copy-start(s32[192]{0:T(256)} %compare_select_fusion) | copy-start | bytes 2308
  157.9 2.8 %copy-start.79 = (bf16[27,192,16]{1,2,0:T(8,128)(2,1)S(1)}, bf16[27,192,16]{1,2,0:T(8,128)(2,1)}, u32[]{:S(2)}) copy-start(bf16[27,192,16]{1,2,0:T(8,128)(2,1)} %param.19) | copy-start | bytes 497668
  158.3 4.0 %copy-start.82 = (pred[2]{0:T(512)(128)(4,1)S(1)}, pred[2]{0:T(512)(128)(4,1)}, u32[]{:S(2)}) copy-start(pred[2]{0:T(512)(128)(4,1)} %copy-done.81) | copy-start | bytes 10
  158.3 4.0 %copy-start.84 = (pred[2]{0:T(512)(128)(4,1)S(1)}, pred[2]{0:T(512)(128)(4,1)}, u32[]{:S(2)}) copy-start(pred[2]{0:T(512)(128)(4,1)} %copy-done.83) | copy-start | bytes 10
  158.8 2.9 %collective-permute-start.2 = (bf16[2,16,24,192]{3,2,1,0:T(8,128)(2,1)S(1)}, bf16[2,16,24,192]{3,2,1,0:T(8,128)(2,1)S(1)}, u32[]{:S(2)}, u32[]{:S(2)}) collective-permute-start(bf16[2,16,24,192]{3,2,1,0:T(8,128)(2,1)S(1)} %fusion.30), channel_id=1, source_target_pairs={{0,1},{1,2},{2,3},{3,4},{4,5},{5,6},{6,7},{7,8},{8,9},{9,10},{10,1... | collective-permute-start | bytes 884744 | tf_op jit(solution)/shard_map/ppermute | solution.py:10
  (46 other events, 46.8 us)
Sparse Core Ops, SparseCore 0:
  9.6 48.1 all-gather.3
  60.1 43.7 all-gather.5
where the time goes:
time: 209 us; the launch traced here: 207 us
  local copies, waits for them, and re-layouts  85.2 us (41%)
  waiting for transfers between devices  37.6 us (18%)
  matrix products  25.9 us (12%)
  blocking collectives  25.7 us (12%)
  between operations  14.8 us (7%)
  other arithmetic  10.9 us (5%)
  starting transfers between devices  7.23 us (3%)
    unnamed x234, local copies, waits for them, and re-layouts  51.5 us
    all_gather x2, waiting for transfers between devices, conv_columns(): lax.all_gather(weight_shard, 'ctx', axis=2, tiled=True)  36 us
    all_gather x1, blocking collectives, body(): all_patches = lax.all_gather(patches, 'ctx', axis=0, tiled=True)  25.7 us
    dot_general x81, matrix products, conv_block(): jnp.dot(shifted, weight[frame_tap * 9 + row_tap * 3 + col_tap], preferred...  25.3 us
    slice x4, local copies, waits for them, and re-layouts, conv_block(): weight[frame_tap * 9 + row_tap * 3 + col_tap]  23 us
    slice x8, local copies, waits for them, and re-layouts, conv_block(): source[:, row_tap:row_tap + height, col_tap:col_tap + breadth, :]  7.41 us
    ppermute x3, starting transfers between devices, shifted_2(): lax.ppermute(value, axis, [(source, source + steps) for source in range(f...  7.19 us
  transfers between devices with their start and end apart: 5, of which 2 were waited for; matrix products, arithmetic and copies ran while one was open for 46% of the time, Pallas kernels for 0%

commit v1 on v0

v1 whole, which is shorter than its diff:
```python
import functools

import jax
import jax.numpy as jnp
import numpy as np
from jax import lax
from jax.experimental import pallas as pl
from jax.experimental.pallas import tpu as pltpu
from jax.sharding import PartitionSpec as P

MESH = pl.DeviceIdType.MESH
ROWS = 16
EPS = 1e-06


def ring_chip(place, chips):
    half = chips // 2
    return jnp.where(place < half, 2 * place, 2 * (chips - 1 - place) + 1)


def ring_place(chip, chips):
    return jnp.where(chip % 2 == 0, chip // 2, chips - 1 - chip // 2)


def rms_silu(values, gain):
    mean = jnp.sum(values * values, axis=-1, keepdims=True) * (1.0 / values.shape[-1])
    normed = values * lax.rsqrt(mean + EPS) * gain
    return (normed / (1.0 + jnp.exp(-normed))).astype(jnp.bfloat16)


def nt_dot(left, right):
    return lax.dot_general(left, right, (((1,), (1,)), ((), ())), preferred_element_type=jnp.float32)


def block_kernel(
    n, frames, height, breadth,
    clip_ref, features_ref, gain1_ref, gain2_ref, gain3_ref, own1_ref, own2_ref, out_w_ref,
    place_ref, tok_ref, pool_ref, keep_ref,
    ordered_ref,
    gathered, halo, acts, taps, latent, patches, final,
    ring_send, ring_recv, pair_send, pair_recv, local_sem, halo_send, halo_recv,
    patch_send, patch_recv, fwd_send, fwd_recv,
):
    me = lax.axis_index("ctx")
    core, chip = lax.rem(me, 2), lax.div(me, 2)
    chips = n // 2
    place = ring_place(chip, chips)
    partner = me + 1 - 2 * core
    follower = lax.rem(me + 1, n)
    size = height * breadth
    channels = features_ref.shape[1]
    depth = 9 * channels
    lanes = taps.shape[2]

    def at(offset):
        return ring_chip(lax.rem(place + offset + chips, chips), chips) * 2 + core

    barrier = pltpu.get_barrier_semaphore()
    for step in range(1, n):
        pl.semaphore_signal(
            barrier, inc=1, device_id={"ctx": lax.rem(me + step, n)}, device_id_type=MESH
        )
    pl.semaphore_wait(barrier, n - 1)

    owns = (own1_ref, own2_ref)

    def ring_copy(w, way, step):
        origin = at(-step) if way == 0 else at(step)
        target = at(1) if way == 0 else at(-1)
        source = owns[w] if step == 0 else gathered.at[w, origin]
        return pltpu.make_async_remote_copy(
            src_ref=source, dst_ref=gathered.at[w, origin],
            send_sem=ring_send.at[w, way, step], recv_sem=ring_recv.at[w, way, step],
            device_id={"ctx": target}, device_id_type=MESH,
        )

    def pair_copy(w, slot, origin):
        source = owns[w] if slot == 0 else gathered.at[w, origin]
        return pltpu.make_async_remote_copy(
            src_ref=source, dst_ref=gathered.at[w, origin],
            send_sem=pair_send.at[w, slot], recv_sem=pair_recv.at[w, slot],
            device_id={"ctx": partner}, device_id_type=MESH,
        )

    reach = (chips // 2, (chips - 1) // 2)

    def begin(w):
        for way in range(2):
            if reach[way] > 0:
                ring_copy(w, way, 0).start()
        pair_copy(w, 0, me).start()

    def advance(w, step):
        for way in range(2):
            if step < reach[way]:
                ring_copy(w, way, step).wait_recv()
                if step + 1 < reach[way]:
                    ring_copy(w, way, step + 1).start()
                origin = at(-step - 1) if way == 0 else at(step + 1)
                pair_copy(w, 1 + 2 * step + way, origin).start()

    def finish(w):
        for way in range(2):
            for step in range(reach[way]):
                ring_copy(w, way, step).wait_send()
        pair_copy(w, 0, me).wait()
        for way in range(2):
            for step in range(reach[way]):
                origin = at(-step - 1) if way == 0 else at(step + 1)
                pair_copy(w, 1 + 2 * step + way, origin).wait()

    def halo_copy(which):
        return pltpu.make_async_remote_copy(
            src_ref=features_ref if which == 0 else acts.at[which - 1],
            dst_ref=halo.at[which],
            send_sem=halo_send.at[which], recv_sem=halo_recv.at[which],
            device_id={"ctx": follower}, device_id_type=MESH,
        )

    halo_copy(0).start()
    begin(0)
    locals_ = [pltpu.make_async_copy(owns[w], gathered.at[w, me], local_sem.at[w]) for w in range(2)]
    for copy in locals_:
        copy.start()

    def kept(tap, frame):
        position = me * frames + frame - 2 + tap
        seen = clip_ref[jnp.maximum(position, 0)]
        same = jnp.logical_and(position >= 0, seen == clip_ref[me * frames + frame])
        return jnp.where(same, 1.0, 0.0)

    columns = lax.broadcasted_iota(jnp.int32, (height, breadth, channels), 1).reshape(size, channels)

    def lay(values, frame_in):
        wide = values.astype(jnp.float32)
        shifted = (
            jnp.where(columns == 0, 0.0, pltpu.roll(wide, 1, 0)),
            wide,
            jnp.where(columns == breadth - 1, 0.0, pltpu.roll(wide, size - 1, 0)),
        )
        for col_tap in range(3):
            for frame in range(frames):
                tap = frame_in - frame
                if 0 <= tap <= 2:
                    piece = shifted[col_tap]
                    if tap < 2:
                        piece = piece * kept(tap, frame)
                    start = (tap * 3 + col_tap) * channels
                    taps[frame, :, start : start + channels] = piece.astype(jnp.bfloat16)

    for frame in range(frames):
        taps[frame, :, depth:] = jnp.zeros((size, lanes - depth), jnp.bfloat16)

    def spread(parts):
        up, mid, down = parts
        zero = jnp.zeros((breadth, mid.shape[1]), jnp.float32)
        return (
            mid
            + jnp.concatenate([zero, up[: size - breadth]], axis=0)
            + jnp.concatenate([down[breadth:], zero], axis=0)
        )

    def conv(frame, weight_of):
        left = taps[frame]
        return spread([nt_dot(left, weight_of(row_tap)) for row_tap in range(3)])

    def gathered_weight(w):
        def weight_of(row_tap):
            part = gathered[w, :, :, row_tap * lanes : (row_tap + 1) * lanes]
            return part.reshape(n * ROWS, lanes)
        return weight_of

    def out_weight(row_tap):
        part = out_w_ref[:, row_tap * lanes : (row_tap + 1) * lanes]
        return jnp.concatenate([part] * 8, axis=0)

    def compact(values):
        return jnp.dot(values, place_ref[...], preferred_element_type=jnp.float32)

    gain1, gain2, gain3 = gain1_ref[...], gain2_ref[...], gain3_ref[...]

    def rows_of(frame):
        return slice(frame * size, (frame + 1) * size)

    for frame in range(frames):
        lay(rms_silu(features_ref[rows_of(frame), :].astype(jnp.float32), gain1), 2 + frame)
    advance(0, 0)
    halo_copy(0).wait()
    for frame in range(2):
        lay(rms_silu(halo[0, rows_of(frame), :].astype(jnp.float32), gain1), frame)
    for step in range(1, reach[0]):
        if step == reach[0] - 1:
            begin(1)
        advance(0, step)
    if reach[0] < 2:
        begin(1)
    for copy in locals_:
        copy.wait()
    finish(0)

    for frame in range(frames):
        first = compact(conv(frame, gathered_weight(0)).astype(jnp.bfloat16))
        acts[0, rows_of(frame), :] = rms_silu(first, gain2)
        if frame < reach[0]:
            advance(1, frame)
    halo_copy(1).start()
    for frame in range(frames):
        lay(acts[0, rows_of(frame), :], 2 + frame)
    for step in range(frames, reach[0] - 1):
        advance(1, step)
    halo_copy(1).wait()
    for frame in range(2):
        lay(halo[1, rows_of(frame), :], frame)
    for step in range(max(frames, reach[0] - 1), reach[0]):
        advance(1, step)
    finish(1)

    for frame in range(frames):
        base = nt_dot(features_ref[rows_of(frame), :], place_ref[...])
        block = compact((base + conv(frame, gathered_weight(1))).astype(jnp.bfloat16))
        acts[1, rows_of(frame), :] = rms_silu(block, gain3)
    halo_copy(2).start()
    for frame in range(frames):
        lay(acts[1, rows_of(frame), :], 2 + frame)
    halo_copy(2).wait()
    for frame in range(2):
        lay(halo[2, rows_of(frame), :], frame)
    for frame in range(frames):
        latent[rows_of(frame), :] = conv(frame, out_weight).astype(jnp.bfloat16) * keep_ref[rows_of(frame), :]
    patches[...] = jnp.dot(
        pool_ref[...], latent[...], preferred_element_type=jnp.float32
    ).astype(jnp.bfloat16)

    def patch_copy(step):
        return pltpu.make_async_remote_copy(
            src_ref=patches, dst_ref=final.at[me],
            send_sem=patch_send.at[step], recv_sem=patch_recv.at[step],
            device_id={"ctx": lax.rem(me + 2 * step, n)}, device_id_type=MESH,
        )

    def forward_copy(step):
        origin = lax.rem(me + n - 2 * step, n)
        return pltpu.make_async_remote_copy(
            src_ref=patches if step == 0 else final.at[origin], dst_ref=final.at[origin],
            send_sem=fwd_send.at[step], recv_sem=fwd_recv.at[step],
            device_id={"ctx": partner}, device_id_type=MESH,
        )

    order = sorted(range(1, chips), key=lambda step: min(step, chips - step))
    for step in reversed(order):
        patch_copy(step).start()
    forward_copy(0).start()
    mine = pltpu.make_async_copy(patches, final.at[me], local_sem.at[2])
    mine.start()
    for step in order:
        patch_copy(step).wait_recv()
        forward_copy(step).start()
    mine.wait()
    for step in order:
        patch_copy(step).wait_send()
    for step in range(chips):
        forward_copy(step).wait()

    packed = final.shape[1]
    count = tok_ref.shape[0]
    device = lax.broadcasted_iota(jnp.int32, (count, packed), 1)
    lane = lax.broadcasted_iota(jnp.int32, (count, final.shape[2]), 1)
    half = final.shape[2] // 2
    tok = tok_ref[...]
    low = jnp.zeros((count, final.shape[2]), jnp.float32)
    high = low
    for owner in range(n):
        rows = final[owner]
        at_low = jnp.where(tok == device + owner * 2 * packed, 1.0, 0.0).astype(jnp.bfloat16)
        at_high = jnp.where(tok == device + (owner * 2 + 1) * packed, 1.0, 0.0).astype(jnp.bfloat16)
        low = low + jnp.dot(at_low, rows, preferred_element_type=jnp.float32)
        high = high + jnp.dot(at_high, rows, preferred_element_type=jnp.float32)
    ordered_ref[...] = jnp.where(lane < half, low, high).astype(jnp.bfloat16)


def modulate_kernel(ordered_ref, embed_ref, shift_ref, scale_ref, out_ref):
    embed = embed_ref[...]
    both = jnp.concatenate([embed, embed], axis=0)
    embedded = jnp.dot(ordered_ref[...], both, preferred_element_type=jnp.float32)
    inverse = 1.0 / embedded.shape[1]
    center = jnp.sum(embedded, axis=-1, keepdims=True) * inverse
    centered = embedded - center
    variance = jnp.sum(centered * centered, axis=-1, keepdims=True) * inverse
    normed = centered * lax.rsqrt(variance + EPS)
    out_ref[...] = (normed * (1.0 + scale_ref[...]) + shift_ref[...]).astype(jnp.bfloat16)


def prepare(weight, lanes, rows):
    channels, outs = weight.shape[1], weight.shape[2]
    split = weight.reshape(3, 3, 3, channels, outs).transpose(4, 1, 0, 2, 3)
    split = split.reshape(outs, 3, 9 * channels)
    padded = jnp.pad(split, ((0, rows - outs), (0, 0), (0, lanes - 9 * channels)))
    return padded.reshape(rows, 3 * lanes)


def body(
    n,
    features, clip_ids, gain_first, weight_first, gain_second, weight_second, gain_third,
    weight_out, embed_weight, shift_mod, scale_mod, token_order,
):
    frames, height, breadth, channels = features.shape
    per, latents = weight_first.shape[2], weight_out.shape[2]
    size = height * breadth
    lanes = -(-9 * channels // 256) * 256
    count = token_order.shape[0]
    width = embed_weight.shape[1]
    patches = frames * size // 4
    packed = patches // 2

    place = np.zeros((n * ROWS, channels), np.float32)
    for channel in range(channels):
        place[channel // per * ROWS + channel % per, channel] = 1
    f, i, j = np.meshgrid(np.arange(frames), np.arange(height), np.arange(breadth), indexing="ij")
    patch = ((f * (height // 2) + i // 2) * (breadth // 2) + j // 2).reshape(-1)
    quarter = (2 * (i % 2) + j % 2).reshape(-1)
    pool = (patch[None, :] % packed == np.arange(packed)[:, None]).astype(np.float32)
    group = np.arange(8 * latents) // latents
    keep = (group[None, :] == (patch // packed * 4 + quarter)[:, None]).astype(np.float32)

    chips = n // 2
    hops = max(1, chips // 2)
    vmem = pl.BlockSpec(memory_space=pltpu.VMEM)
    dma = pltpu.SemaphoreType.DMA
    ordered = pl.pallas_call(
        functools.partial(block_kernel, n, frames, height, breadth),
        out_shape=jax.ShapeDtypeStruct((count, 8 * latents), jnp.bfloat16),
        in_specs=[pl.BlockSpec(memory_space=pltpu.SMEM)] + [vmem] * 11,
        out_specs=vmem,
        scratch_shapes=[
            pltpu.VMEM((2, n, ROWS, 3 * lanes), jnp.bfloat16),
            pltpu.VMEM((3, frames * size, channels), jnp.bfloat16),
            pltpu.VMEM((2, frames * size, channels), jnp.bfloat16),
            pltpu.VMEM((frames, size, lanes), jnp.bfloat16),
            pltpu.VMEM((frames * size, 8 * latents), jnp.bfloat16),
            pltpu.VMEM((packed, 8 * latents), jnp.bfloat16),
            pltpu.VMEM((n, packed, 8 * latents), jnp.bfloat16),
            dma((2, 2, hops)), dma((2, 2, hops)),
            dma((2, 2 * hops + 1)), dma((2, 2 * hops + 1)),
            dma((3,)), dma((3,)), dma((3,)),
            dma((chips,)), dma((chips,)), dma((chips,)), dma((chips,)),
        ],
        compiler_params=pltpu.CompilerParams(
            collective_id=0, has_side_effects=True, vmem_limit_bytes=60 * 1024 * 1024
        ),
        name="block",
    )(
        clip_ids, features.reshape(frames * size, channels),
        gain_first.reshape(1, channels), gain_second.reshape(1, channels),
        gain_third.reshape(1, channels),
        prepare(weight_first, lanes, ROWS), prepare(weight_second, lanes, ROWS),
        prepare(weight_out, lanes, latents),
        jnp.asarray(place, jnp.bfloat16), token_order.reshape(count, 1),
        jnp.asarray(pool, jnp.bfloat16), jnp.asarray(keep, jnp.bfloat16),
    )
    tile = count // 4
    return pl.pallas_call(
        modulate_kernel,
        out_shape=jax.ShapeDtypeStruct((count, width), jnp.bfloat16),
        grid=(count // tile,),
        in_specs=[
            pl.BlockSpec((tile, 8 * latents), lambda step: (step, 0)),
            pl.BlockSpec((embed_weight.shape[0], width), lambda step: (0, 0)),
            pl.BlockSpec((1, width), lambda step: (0, 0)),
            pl.BlockSpec((1, width), lambda step: (0, 0)),
        ],
        out_specs=pl.BlockSpec((tile, width), lambda step: (step, 0)),
        name="modulate",
    )(ordered, embed_weight, shift_mod.reshape(1, width), scale_mod.reshape(1, width))


def solution(mesh):
    in_specs = (
        P(("groups", "ctx"), None, None, None),
        P("groups"),
        P(),
        P(None, None, "ctx"),
        P(),
        P(None, None, "ctx"),
        P(),
        P(),
        P(),
        P(),
        P(),
        P(("groups", "ctx")),
    )
    out_specs = P(("groups", "ctx"), None)
    return jax.shard_map(
        functools.partial(body, mesh.shape["ctx"]),
        mesh=mesh, in_specs=in_specs, out_specs=out_specs, check_vma=False,
    )
```

time: 209 us -> 89.2 us (0.43)
  Pallas kernels: 0 us -> 82.8 us
  local copies, waits for them, and re-layouts: 85.2 us -> 6 us
  waiting for transfers between devices: 37.6 us -> 0 us
  matrix products: 25.9 us -> 0 us
  blocking collectives: 25.7 us -> 0 us
  between operations: 14.8 us -> 0.09 us
  other arithmetic: 10.9 us -> 0 us
  starting transfers between devices: 7.23 us -> 0 us
    pallas_call x0 -> x2, Pallas kernels: none -> 82.8 us  [the longest x1 78.5 us: body(): pl.pallas_call(functools.partial(block_kernel, n, frames, height, breadth...]
    unnamed x234 -> x8, local copies, waits for them, and re-layouts: 51.5 us -> 2.19 us
    all_gather x2 -> x0, waiting for transfers between devices: 36 us -> none  [conv_columns(): lax.all_gather(weight_shard, 'ctx', axis=2, tiled=True)]
    slice x12 -> x0, local copies, waits for them, and re-layouts: 30.4 us -> none  [the longest x4 23 us: conv_block(): weight[frame_tap * 9 + row_tap * 3 + col_tap]]
    dot_general x82 -> x0, matrix products: 25.9 us -> none  [the longest x81 25.3 us: conv_block(): jnp.dot(shifted, weight[frame_tap * 9 + row_tap * 3 + col_tap], preferred...]
    all_gather x1 -> x0, blocking collectives: 25.7 us -> none  [body(): all_patches = lax.all_gather(patches, 'ctx', axis=0, tiled=True)]
    ppermute x3 -> x0, starting transfers between devices: 7.19 us -> none  [shifted_2(): lax.ppermute(value, axis, [(source, source + steps) for source in range(f...]
    convert_element_type x4 -> x0, other arithmetic: 3.43 us -> none  [the longest x3 1.91 us: rms_silu(): return jax.nn.silu(normed).astype(jnp.bfloat16)]
  transfers between devices with their start and end apart: 5 -> 0, of which waited for: 2 -> 0; matrix products, arithmetic and copies ran while one was open for 46% -> 0% of each run, Pallas kernels for 0% -> 0%
where the time goes in v1:
time: 89.2 us; the launch traced here: 88.9 us
  Pallas kernels  82.8 us (93%)
  local copies, waits for them, and re-layouts  6 us (7%)
    pallas_call x1, Pallas kernels, body(): pl.pallas_call(functools.partial(block_kernel, n, frames, height, breadth...  78.5 us
    pallas_call x1, Pallas kernels, body(): pl.pallas_call(modulate_kernel, out_shape=jax.ShapeDtypeStruct((count, wi...  4.26 us
    unnamed x8, local copies, waits for them, and re-layouts  2.19 us

profile of v1, /device:TPU:0, one launch (start us, length us, event | category | flops | bytes accessed | tf_op | source)
XLA Modules:
  0.0 88.9 jit_solution(9463071301841040221)
XLA Ops:
  0.0 0.0 copy-start.1
  0.0 1.5 %copy.23.tok_ref = s32[192,1]{1,0:T(8,128)} copy(s32[192,1]{0,1:T(1,128)} %bitcast.38) | data formatting | bytes 1536 | tf_op jit(solution)/shard_map/reshape | solution.py:357
  1.5 1.0 %reshape.52 = bf16[3,3,3,192,12]{3,2,1,0,4:T(4,128)(2,1)S(1)} reshape(bf16[27,192,12]{1,0,2:T(8,128)(2,1)} %param.18) | data formatting | bytes 248832 | tf_op jit(solution)/shard_map/reshape | solution.py:295
  2.5 0.1 copy.19
  2.6 0.2 reshape.53
  2.8 0.1 pad.11
  2.9 0.0 copy-start
  2.9 0.7 copy.25
  3.6 0.0 copy-done.1
  3.6 0.1 reshape.55
  3.7 0.1 copy.20
  3.8 0.2 reshape.56
  4.0 0.1 pad.12
  4.1 0.7 copy.26
  4.8 0.0 copy-done
  4.8 0.2 copy.29
  5.0 0.2 reshape.59
  5.2 0.1 copy.24
  5.3 0.1 pad.13.clone
  5.4 0.7 copy.27
  6.1 78.5 %block.1.ordered_ref = bf16[192,128]{1,0:T(8,128)(2,1)} custom-call(s32[32]{0:T(128)} %clip_ref.1, bf16[768,192]{1,0:T(8,128)(2,1)} %bitcast.34, f32[1,192]{1,0:T(1,128)} %bitcast.39, f32[1,192]{1,0:T(1,128)} %bitcast.40, f32[1,192]{1,0:T(1,128)} %bitcast.41, bf16[16,5376]{1,0:T(8,128)(2,1)} %bitcast.31, bf16[16,5376]{1,0:T(8,128)(2,1)} %bitcast.32, ...), custom_call_target="tpu_custom_call" | custom-call | tf_op jit(solution)/shard_map/block/pallas_call | solution.py:329
  84.6 4.3 %modulate.1 = bf16[192,3072]{1,0:T(8,128)(2,1)} custom-call(bf16[192,128]{1,0:T(8,128)(2,1)} %block.1.ordered_ref, bf16[64,3072]{1,0:T(8,128)(2,1)} %embed_ref.1, f32[1,3072]{1,0:T(1,128)} %bitcast.36, f32[1,3072]{1,0:T(1,128)} %bitcast.37), custom_call_target="tpu_custom_call" | custom-call | tf_op jit(solution)/shard_map/modulate/pallas_call | solution.py:361
Async XLA Ops:
  0.0 3.6 %copy-start.1 = (bf16[27,192,12]{1,0,2:T(8,128)(2,1)S(1)}, bf16[27,192,12]{1,0,2:T(8,128)(2,1)}, u32[]{:S(2)}) copy-start(bf16[27,192,12]{1,0,2:T(8,128)(2,1)} %param.20) | copy-start | bytes 373252
  2.9 1.9 %copy-start = (bf16[27,192,16]{1,2,0:T(8,128)(2,1)S(1)}, bf16[27,192,16]{1,2,0:T(8,128)(2,1)}, u32[]{:S(2)}) copy-start(bf16[27,192,16]{1,2,0:T(8,128)(2,1)} %param.22) | copy-start | bytes 497668

commit v2 on v1

v2 whole, which is shorter than its diff:
```python
import functools

import jax
import jax.numpy as jnp
import numpy as np
from jax import lax
from jax.experimental import pallas as pl
from jax.experimental.pallas import tpu as pltpu
from jax.sharding import PartitionSpec as P

MESH = pl.DeviceIdType.MESH
EPS = 1e-06


def ring_chip(place, chips):
    half = chips // 2
    return jnp.where(place < half, 2 * place, 2 * (chips - 1 - place) + 1)


def ring_place(chip, chips):
    return jnp.where(chip % 2 == 0, chip // 2, chips - 1 - chip // 2)


def rms_silu(values, gain):
    mean = jnp.sum(values * values, axis=-1, keepdims=True) * (1.0 / values.shape[-1])
    normed = values * lax.rsqrt(mean + EPS) * gain
    return (normed / (1.0 + jnp.exp(-normed))).astype(jnp.bfloat16)


def nt_dot(left, right):
    return lax.dot_general(left, right, (((1,), (1,)), ((), ())), preferred_element_type=jnp.float32)


def block_kernel(
    n, pairs, per, frames, height, breadth,
    clip_ref, features_ref, gain1_ref, gain2_ref, gain3_ref, own1_ref, own2_ref, out_w_ref,
    place_ref, tok_ref, pool_ref, keep_ref,
    ordered_ref,
    gathered, halo, acts, taps, latent, patches, final,
    ring_send, ring_recv, cross_send, cross_recv, pair_send, pair_recv, local_sem,
    halo_send, halo_recv, patch_send, patch_recv, fwd_send, fwd_recv,
):
    me = lax.axis_index("ctx")
    group = lax.axis_index("groups")
    core, chip = lax.rem(me, 2), lax.div(me, 2)
    parity = lax.rem(group, 2)
    chips = n // 2
    place = ring_place(chip, chips)
    partner = me + 1 - 2 * core
    follower = lax.rem(me + 1, n)
    size = height * breadth
    channels = features_ref.shape[1]
    depth = 9 * channels
    lanes = taps.shape[2]
    rows = gathered.shape[3]
    split = gathered.shape[4] > lanes

    def at(offset):
        return ring_chip(lax.rem(place + offset + chips, chips), chips) * 2 + core

    def rows_of(frame):
        return slice(frame * size, (frame + 1) * size)

    def pack(values, which, frame):
        over = values[:, 128:]
        acts[which, frame, :size, :] = values[:, :128].astype(jnp.bfloat16)
        both = jnp.concatenate([over[: size // 2], over[size // 2 :]], axis=1)
        acts[which, frame, size:, :] = both.astype(jnp.bfloat16)

    def unpack(which, frame):
        both = halo[which, frame, size:, :].astype(jnp.float32)
        over = jnp.concatenate([both[:, : channels - 128], both[:, channels - 128 :]], axis=0)
        return jnp.concatenate([halo[which, frame, :size, :].astype(jnp.float32), over], axis=1)

    for w, own in enumerate((own1_ref, own2_ref)):
        for part in range(3):
            values = own[:, part * lanes : (part + 1) * lanes]
            if split:
                rest = values.astype(jnp.float32)[rows:]
                rest = rest[:, : lanes // 2] + pltpu.roll(rest[:, lanes // 2 :], rows // 2, 0)
                gathered[w, me, part, :, lanes:] = rest.astype(jnp.bfloat16)
            gathered[w, me, part, :, :lanes] = values[:rows]
    for frame in range(frames):
        pack(features_ref[rows_of(frame), :].astype(jnp.float32), 0, frame)

    barrier = pltpu.get_barrier_semaphore()
    for step in range(1, n):
        pl.semaphore_signal(
            barrier, inc=1, device_id={"ctx": lax.rem(me + step, n)}, device_id_type=MESH
        )
    if pairs:
        peer = group + 1 - 2 * parity
        pl.semaphore_signal(barrier, inc=1, device_id={"groups": peer}, device_id_type=MESH)
    pl.semaphore_wait(barrier, n if pairs else n - 1)

    half_way = chips // 2
    if pairs:
        ring_parts = (0, 1 + parity)
        cross_part = 2 - parity
        reach = ((half_way, chips - 1 - half_way), (chips - 1 - half_way, half_way))
    else:
        ring_parts = (0, 1, 2)
        reach = ((half_way, chips - 1 - half_way),) * 3
    hops = ring_send.shape[3]
    last = len(ring_parts) - 1

    def origin_of(way, step):
        return at(-step - 1) if way == 0 else at(step + 1)

    def ring_copy(w, k, way, step):
        block = gathered.at[w, me if step == 0 else origin_of(way, step - 1), ring_parts[k]]
        return pltpu.make_async_remote_copy(
            src_ref=block, dst_ref=block,
            send_sem=ring_send.at[w, k, way, step], recv_sem=ring_recv.at[w, k, way, step],
            device_id={"ctx": at(1) if way == 0 else at(-1)}, device_id_type=MESH,
        )

    def cross_copy(w, way, step, part):
        block = gathered.at[w, origin_of(way, step), part]
        return pltpu.make_async_remote_copy(
            src_ref=block, dst_ref=block,
            send_sem=cross_send.at[w, way, step], recv_sem=cross_recv.at[w, way, step],
            device_id={"groups": peer}, device_id_type=MESH,
        )

    def own_pair(w):
        block = gathered.at[w, me]
        return pltpu.make_async_remote_copy(
            src_ref=block, dst_ref=block,
            send_sem=pair_send.at[w, 0], recv_sem=pair_recv.at[w, 0],
            device_id={"ctx": partner}, device_id_type=MESH,
        )

    def pair_copy(w, k, way, step):
        part = ring_parts[k] if k <= last else cross_part
        block = gathered.at[w, origin_of(way, step), part]
        slot = 1 + (k * 2 + way) * hops + step
        return pltpu.make_async_remote_copy(
            src_ref=block, dst_ref=block,
            send_sem=pair_send.at[w, slot], recv_sem=pair_recv.at[w, slot],
            device_id={"ctx": partner}, device_id_type=MESH,
        )

    def begin(w):
        for k in range(last, -1, -1):
            for way in range(2):
                if reach[k][way] > 0:
                    ring_copy(w, k, way, 0).start()
        own_pair(w).start()

    def arrive(w, step):
        if pairs and step >= 0:
            for way in range(2):
                if step < reach[last][way]:
                    cross_copy(w, way, step, cross_part).wait_recv()
                    pair_copy(w, last + 1, way, step).start()

    def advance(w, step):
        for k in range(last, -1, -1):
            for way in range(2):
                if step < reach[k][way]:
                    ring_copy(w, k, way, step).wait_recv()
                    if step + 1 < reach[k][way]:
                        ring_copy(w, k, way, step + 1).start()
                    if pairs and k == last:
                        cross_copy(w, way, step, ring_parts[k]).start()
                    pair_copy(w, k, way, step).start()
        arrive(w, step - 1)

    def finish(w):
        arrive(w, half_way - 1)
        own_pair(w).wait()
        for k in range(last + 1):
            for way in range(2):
                for step in range(reach[k][way]):
                    ring_copy(w, k, way, step).wait_send()
                    if pairs and k == last:
                        cross_copy(w, way, step, ring_parts[k]).wait_send()
                        pair_copy(w, k + 1, way, step).wait()
                    pair_copy(w, k, way, step).wait()

    def halo_copy(which, frame):
        return pltpu.make_async_remote_copy(
            src_ref=acts.at[which, frame], dst_ref=halo.at[which, frame],
            send_sem=halo_send.at[which, frame], recv_sem=halo_recv.at[which, frame],
            device_id={"ctx": follower}, device_id_type=MESH,
        )

    begin(0)
    for frame in range(frames):
        halo_copy(0, frame).start()

    def kept(tap, frame):
        position = me * frames + frame - 2 + tap
        seen = clip_ref[jnp.maximum(position, 0)]
        same = jnp.logical_and(position >= 0, seen == clip_ref[me * frames + frame])
        return jnp.where(same, 1.0, 0.0)

    columns = lax.broadcasted_iota(jnp.int32, (height, breadth, channels), 1).reshape(size, channels)

    def lay(values, frame_in):
        wide = values.astype(jnp.float32)
        shifted = (
            jnp.where(columns == 0, 0.0, pltpu.roll(wide, 1, 0)),
            wide,
            jnp.where(columns == breadth - 1, 0.0, pltpu.roll(wide, size - 1, 0)),
        )
        for col_tap in range(3):
            for frame in range(frames):
                tap = frame_in - frame
                if 0 <= tap <= 2:
                    piece = shifted[col_tap]
                    if tap < 2:
                        piece = piece * kept(tap, frame)
                    start = (tap * 3 + col_tap) * channels
                    taps[frame, :, start : start + channels] = piece.astype(jnp.bfloat16)

    for frame in range(frames):
        taps[frame, :, depth:] = jnp.zeros((size, lanes - depth), jnp.bfloat16)

    def spread(parts):
        up, mid, down = parts
        zero = jnp.zeros((breadth, mid.shape[1]), jnp.float32)
        return (
            mid
            + jnp.concatenate([zero, up[: size - breadth]], axis=0)
            + jnp.concatenate([down[breadth:], zero], axis=0)
        )

    def conv(frame, w):
        if not split:
            left = taps[frame]
            return spread([
                nt_dot(left, gathered[w, :, part].reshape(n * rows, lanes)) for part in range(3)
            ])
        halves = []
        for half in range(2):
            span = slice(half * lanes // 2, (half + 1) * lanes // 2)
            left = taps[frame, :, span]
            sums = []
            for part in range(3):
                main = gathered[w, :, part, :, span].reshape(n * rows, lanes // 2)
                rest = gathered[w, :, part, :, lanes:].reshape(n * rows, lanes // 2)
                sums.append(nt_dot(left, jnp.concatenate([main, rest], axis=0)))
            halves.append(spread(sums))
        own, other = halves
        edge = n * rows
        moved = pltpu.roll(other[:, edge:], edge - rows // 2, 1)
        return jnp.concatenate([own[:, :edge] + other[:, :edge], own[:, edge:] + moved], axis=1)

    def out_weight(row_tap):
        part = out_w_ref[:, row_tap * lanes : (row_tap + 1) * lanes]
        return jnp.concatenate([part] * 8, axis=0)

    def compact(values):
        return jnp.dot(values, place_ref[...], preferred_element_type=jnp.float32)

    gain1, gain2, gain3 = gain1_ref[...], gain2_ref[...], gain3_ref[...]

    for frame in range(frames):
        lay(rms_silu(features_ref[rows_of(frame), :].astype(jnp.float32), gain1), 2 + frame)
    advance(0, 0)
    for frame in range(frames):
        halo_copy(0, frame).wait()
        lay(rms_silu(unpack(0, frame), gain1), frame)
    for step in range(1, half_way):
        advance(0, step)
        if step == half_way - 2:
            begin(1)
    if half_way < 3:
        begin(1)
    finish(0)

    own = []
    for frame in range(frames):
        first = compact(conv(frame, 0).astype(jnp.bfloat16))
        value = rms_silu(first, gain2)
        pack(value.astype(jnp.float32), 1, frame)
        halo_copy(1, frame).start()
        if frame < half_way:
            advance(1, frame)
        own.append(value)
    for frame in range(frames):
        lay(own[frame], 2 + frame)
    for step in range(frames, half_way):
        advance(1, step)
    for frame in range(frames):
        halo_copy(1, frame).wait()
        lay(unpack(1, frame), frame)
    finish(1)

    own = []
    for frame in range(frames):
        base = nt_dot(features_ref[rows_of(frame), :], place_ref[...])
        block = compact((base + conv(frame, 1)).astype(jnp.bfloat16))
        value = rms_silu(block, gain3)
        pack(value.astype(jnp.float32), 2, frame)
        halo_copy(2, frame).start()
        own.append(value)
    for frame in range(frames):
        lay(own[frame], 2 + frame)
    for frame in range(frames):
        halo_copy(2, frame).wait()
        lay(unpack(2, frame), frame)
    for frame in range(frames):
        left = taps[frame]
        sums = spread([nt_dot(left, out_weight(part)) for part in range(3)])
        latent[rows_of(frame), :] = sums.astype(jnp.bfloat16) * keep_ref[rows_of(frame), :]
    patches[...] = jnp.dot(
        pool_ref[...], latent[...], preferred_element_type=jnp.float32
    ).astype(jnp.bfloat16)

    def patch_copy(step):
        return pltpu.make_async_remote_copy(
            src_ref=patches, dst_ref=final.at[me],
            send_sem=patch_send.at[step], recv_sem=patch_recv.at[step],
            device_id={"ctx": lax.rem(me + 2 * step, n)}, device_id_type=MESH,
        )

    def forward_copy(step):
        origin = lax.rem(me + n - 2 * step, n)
        return pltpu.make_async_remote_copy(
            src_ref=patches if step == 0 else final.at[origin], dst_ref=final.at[origin],
            send_sem=fwd_send.at[step], recv_sem=fwd_recv.at[step],
            device_id={"ctx": partner}, device_id_type=MESH,
        )

    order = sorted(range(1, chips), key=lambda step: min(step, chips - step))
    for step in reversed(order):
        patch_copy(step).start()
    forward_copy(0).start()
    mine = pltpu.make_async_copy(patches, final.at[me], local_sem.at[0])
    mine.start()
    for step in order:
        patch_copy(step).wait_recv()
        forward_copy(step).start()
    mine.wait()
    for step in order:
        patch_copy(step).wait_send()
    for step in range(chips):
        forward_copy(step).wait()

    packed, packed_lanes = final.shape[1], final.shape[2]
    count = tok_ref.shape[1]
    device = lax.broadcasted_iota(jnp.int32, (count, packed), 1)
    lane = lax.broadcasted_iota(jnp.int32, (count, final.shape[2]), 1)
    half = final.shape[2] // 2
    tok = jnp.broadcast_to(tok_ref[...].astype(jnp.float32), (packed_lanes, count)).T[:, :packed]
    tok = tok.astype(jnp.int32)
    low = jnp.zeros((count, final.shape[2]), jnp.float32)
    high = low
    for owner in range(n):
        table = final[owner]
        at_low = jnp.where(tok == device + owner * 2 * packed, 1.0, 0.0).astype(jnp.bfloat16)
        at_high = jnp.where(tok == device + (owner * 2 + 1) * packed, 1.0, 0.0).astype(jnp.bfloat16)
        low = low + jnp.dot(at_low, table, preferred_element_type=jnp.float32)
        high = high + jnp.dot(at_high, table, preferred_element_type=jnp.float32)
    ordered_ref[...] = jnp.where(lane < half, low, high).astype(jnp.bfloat16)


def modulate_kernel(ordered_ref, embed_ref, shift_ref, scale_ref, out_ref):
    embed = embed_ref[...]
    both = jnp.concatenate([embed, embed], axis=0)
    embedded = jnp.dot(ordered_ref[...], both, preferred_element_type=jnp.float32)
    inverse = 1.0 / embedded.shape[1]
    center = jnp.sum(embedded, axis=-1, keepdims=True) * inverse
    centered = embedded - center
    variance = jnp.sum(centered * centered, axis=-1, keepdims=True) * inverse
    normed = centered * lax.rsqrt(variance + EPS)
    out_ref[...] = (normed * (1.0 + scale_ref[...]) + shift_ref[...]).astype(jnp.bfloat16)


def prepare(weight, lanes, rows):
    channels, outs = weight.shape[1], weight.shape[2]
    split = weight.reshape(3, 3, 3, channels, outs).transpose(4, 1, 0, 2, 3)
    split = split.reshape(outs, 3, 9 * channels)
    padded = jnp.pad(split, ((0, rows - outs), (0, 0), (0, lanes - 9 * channels)))
    return padded.reshape(rows, 3 * lanes)


def body(
    n, pairs,
    features, clip_ids, gain_first, weight_first, gain_second, weight_second, gain_third,
    weight_out, embed_weight, shift_mod, scale_mod, token_order,
):
    frames, height, breadth, channels = features.shape
    per, latents = weight_first.shape[2], weight_out.shape[2]
    size = height * breadth
    lanes = -(-9 * channels // 256) * 256
    count = token_order.shape[0]
    width = embed_weight.shape[1]
    patches = frames * size // 4
    packed = patches // 2

    split = per == 12
    rows = 8 if split else -(-per // 8) * 8
    whole_rows = 16 if split else rows
    wide = lanes + lanes // 2 if split else lanes
    place = np.zeros((n * whole_rows, channels), np.float32)
    for channel in range(channels):
        owner, row = divmod(channel, per)
        place[(row // rows * n + owner) * rows + row % rows, channel] = 1
    f, i, j = np.meshgrid(np.arange(frames), np.arange(height), np.arange(breadth), indexing="ij")
    patch = ((f * (height // 2) + i // 2) * (breadth // 2) + j // 2).reshape(-1)
    quarter = (2 * (i % 2) + j % 2).reshape(-1)
    pool = (patch[None, :] % packed == np.arange(packed)[:, None]).astype(np.float32)
    group = np.arange(8 * latents) // latents
    keep = (group[None, :] == (patch // packed * 4 + quarter)[:, None]).astype(np.float32)

    chips = n // 2
    hops = max(1, chips // 2)
    vmem = pl.BlockSpec(memory_space=pltpu.VMEM)
    dma = pltpu.SemaphoreType.DMA
    ordered = pl.pallas_call(
        functools.partial(block_kernel, n, pairs, per, frames, height, breadth),
        out_shape=jax.ShapeDtypeStruct((count, 8 * latents), jnp.bfloat16),
        in_specs=[pl.BlockSpec(memory_space=pltpu.SMEM)] + [vmem] * 11,
        out_specs=vmem,
        scratch_shapes=[
            pltpu.VMEM((2, n, 3, rows, wide), jnp.bfloat16),
            pltpu.VMEM((3, frames, size * 3 // 2, 128), jnp.bfloat16),
            pltpu.VMEM((3, frames, size * 3 // 2, 128), jnp.bfloat16),
            pltpu.VMEM((frames, size, lanes), jnp.bfloat16),
            pltpu.VMEM((frames * size, 8 * latents), jnp.bfloat16),
            pltpu.VMEM((packed, 8 * latents), jnp.bfloat16),
            pltpu.VMEM((n, packed, 8 * latents), jnp.bfloat16),
            dma((2, 3, 2, hops)), dma((2, 3, 2, hops)),
            dma((2, 2, hops)), dma((2, 2, hops)),
            dma((2, 1 + 6 * hops)), dma((2, 1 + 6 * hops)),
            dma((1,)), dma((3, frames)), dma((3, frames)),
            dma((chips,)), dma((chips,)), dma((chips,)), dma((chips,)),
        ],
        compiler_params=pltpu.CompilerParams(
            collective_id=0, has_side_effects=True, vmem_limit_bytes=60 * 1024 * 1024
        ),
        name="block",
    )(
        clip_ids, features.reshape(frames * size, channels),
        gain_first.reshape(1, channels), gain_second.reshape(1, channels),
        gain_third.reshape(1, channels),
        prepare(weight_first, lanes, whole_rows), prepare(weight_second, lanes, whole_rows),
        prepare(weight_out, lanes, latents),
        jnp.asarray(place, jnp.bfloat16), token_order.reshape(1, count),
        jnp.asarray(pool, jnp.bfloat16), jnp.asarray(keep, jnp.bfloat16),
    )
    tile = count // 4
    return pl.pallas_call(
        modulate_kernel,
        out_shape=jax.ShapeDtypeStruct((count, width), jnp.bfloat16),
        grid=(count // tile,),
        in_specs=[
            pl.BlockSpec((tile, 8 * latents), lambda step: (step, 0)),
            pl.BlockSpec((embed_weight.shape[0], width), lambda step: (0, 0)),
            pl.BlockSpec((1, width), lambda step: (0, 0)),
            pl.BlockSpec((1, width), lambda step: (0, 0)),
        ],
        out_specs=pl.BlockSpec((tile, width), lambda step: (step, 0)),
        name="modulate",
    )(ordered, embed_weight, shift_mod.reshape(1, width), scale_mod.reshape(1, width))


def solution(mesh):
    in_specs = (
        P(("groups", "ctx"), None, None, None),
        P("groups"),
        P(),
        P(None, None, "ctx"),
        P(),
        P(None, None, "ctx"),
        P(),
        P(),
        P(),
        P(),
        P(),
        P(("groups", "ctx")),
    )
    out_specs = P(("groups", "ctx"), None)
    return jax.shard_map(
        functools.partial(body, mesh.shape["ctx"], mesh.shape["groups"] % 2 == 0),
        mesh=mesh, in_specs=in_specs, out_specs=out_specs, check_vma=False,
    )
```

time: 89.2 us -> 72.1 us (0.81)
  Pallas kernels: 82.8 us -> 67.2 us
  local copies, waits for them, and re-layouts: 6 us -> 4.57 us
    pallas_call x1, Pallas kernels: 78.5 us -> 62.9 us  [body(): pl.pallas_call(functools.partial(block_kernel, n, pairs, per, frames, hei...]
    reshape x1 -> x0, local copies, waits for them, and re-layouts: 1.47 us -> none  [body(): token_order.reshape(count, 1)]
where the time goes in v2:
time: 72.1 us; the launch traced here: 71.8 us
  Pallas kernels  67.2 us (93%)
  local copies, waits for them, and re-layouts  4.57 us (6%)
    pallas_call x1, Pallas kernels, body(): pl.pallas_call(functools.partial(block_kernel, n, pairs, per, frames, hei...  62.9 us
    pallas_call x1, Pallas kernels, body(): pl.pallas_call(modulate_kernel, out_shape=jax.ShapeDtypeStruct((count, wi...  4.26 us
    unnamed x8, local copies, waits for them, and re-layouts  2.19 us

profile of v2, /device:TPU:0, one launch (start us, length us, event | category | flops | bytes accessed | tf_op | source)
XLA Modules:
  0.0 71.8 jit_solution(15540303561293250506)
XLA Ops:
  0.0 0.0 copy-start.1
  0.0 1.1 %reshape.52 = bf16[3,3,3,192,12]{3,2,1,0,4:T(4,128)(2,1)S(1)} reshape(bf16[27,192,12]{1,0,2:T(8,128)(2,1)} %param.18) | data formatting | bytes 248832 | tf_op jit(solution)/shard_map/reshape | solution.py:375
  1.1 0.1 copy.19
  1.2 0.2 reshape.53
  1.4 0.1 pad.11
  1.5 0.0 copy-start
  1.5 0.7 copy.24
  2.2 0.0 copy-done.1
  2.2 0.1 reshape.55
  2.3 0.1 copy.20
  2.4 0.2 reshape.56
  2.6 0.1 pad.12
  2.7 0.7 copy.25
  3.4 0.0 copy-done
  3.4 0.2 copy.28
  3.5 0.2 reshape.59
  3.7 0.1 copy.23
  3.8 0.1 pad.13.clone
  4.0 0.7 copy.26
  4.7 62.9 %block.1.ordered_ref = bf16[192,128]{1,0:T(8,128)(2,1)} custom-call(s32[32]{0:T(128)} %clip_ref.1, bf16[768,192]{1,0:T(8,128)(2,1)} %bitcast.34, f32[1,192]{1,0:T(1,128)} %bitcast.38, f32[1,192]{1,0:T(1,128)} %bitcast.39, f32[1,192]{1,0:T(1,128)} %bitcast.40, bf16[16,5376]{1,0:T(8,128)(2,1)} %bitcast.31, bf16[16,5376]{1,0:T(8,128)(2,1)} %bitcast.32, ...), custom_call_target="tpu_custom_call" | custom-call | tf_op jit(solution)/shard_map/block/pallas_call | solution.py:414
  67.6 4.3 %modulate.1 = bf16[192,3072]{1,0:T(8,128)(2,1)} custom-call(bf16[192,128]{1,0:T(8,128)(2,1)} %block.1.ordered_ref, bf16[64,3072]{1,0:T(8,128)(2,1)} %embed_ref.1, f32[1,3072]{1,0:T(1,128)} %bitcast.36, f32[1,3072]{1,0:T(1,128)} %bitcast.37), custom_call_target="tpu_custom_call" | custom-call | tf_op jit(solution)/shard_map/modulate/pallas_call | solution.py:447
Async XLA Ops:
  0.0 2.2 %copy-start.1 = (bf16[27,192,12]{1,0,2:T(8,128)(2,1)S(1)}, bf16[27,192,12]{1,0,2:T(8,128)(2,1)}, u32[]{:S(2)}) copy-start(bf16[27,192,12]{1,0,2:T(8,128)(2,1)} %param.20) | copy-start | bytes 373252
  1.5 1.9 %copy-start = (bf16[27,192,16]{1,2,0:T(8,128)(2,1)S(1)}, bf16[27,192,16]{1,2,0:T(8,128)(2,1)}, u32[]{:S(2)}) copy-start(bf16[27,192,16]{1,2,0:T(8,128)(2,1)} %param.22) | copy-start | bytes 497668

commit v3 on v2

--- a/solution.py
+++ b/solution.py
@@ -33,12 +33,12 @@
 
 def block_kernel(
     n, pairs, per, frames, height, breadth,
-    clip_ref, features_ref, gain1_ref, gain2_ref, gain3_ref, own1_ref, own2_ref, out_w_ref,
+    clip_ref, features_ref, gain1_ref, gain2_ref, gain3_ref, own1_ref, own2_ref, raw_out_ref,
     place_ref, tok_ref, pool_ref, keep_ref,
     ordered_ref,
     gathered, halo, acts, taps, latent, patches, final,
     ring_send, ring_recv, cross_send, cross_recv, pair_send, pair_recv, local_sem,
-    halo_send, halo_recv, patch_send, patch_recv, fwd_send, fwd_recv,
+    halo_send, halo_recv, patch_send, patch_recv, fwd_send, fwd_recv, out_w_ref,
 ):
     me = lax.axis_index("ctx")
     group = lax.axis_index("groups")
@@ -72,14 +72,16 @@
         over = jnp.concatenate([both[:, : channels - 128], both[:, channels - 128 :]], axis=0)
         return jnp.concatenate([halo[which, frame, :size, :].astype(jnp.float32), over], axis=1)
 
-    for w, own in enumerate((own1_ref, own2_ref)):
-        for part in range(3):
-            values = own[:, part * lanes : (part + 1) * lanes]
-            if split:
-                rest = values.astype(jnp.float32)[rows:]
-                rest = rest[:, : lanes // 2] + pltpu.roll(rest[:, lanes // 2 :], rows // 2, 0)
-                gathered[w, me, part, :, lanes:] = rest.astype(jnp.bfloat16)
-            gathered[w, me, part, :, :lanes] = values[:rows]
+    def place_own(w, part, values):
+        if split:
+            rest = values.astype(jnp.float32)[rows:]
+            rest = rest[:, : lanes // 2] + pltpu.roll(rest[:, lanes // 2 :], rows // 2, 0)
+            gathered[w, me, part, :, lanes:] = rest.astype(jnp.bfloat16)
+        gathered[w, me, part, :, :lanes] = values[:rows]
+
+    for part in range(3):
+        for w, own in enumerate((own1_ref, own2_ref)):
+            place_own(w, part, own[:, part * lanes : (part + 1) * lanes])
     for frame in range(frames):
         pack(features_ref[rows_of(frame), :].astype(jnp.float32), 0, frame)
 
@@ -257,6 +259,13 @@
 
     gain1, gain2, gain3 = gain1_ref[...], gain2_ref[...], gain3_ref[...]
 
+    for part in range(3):
+        for tap in range(9):
+            start = part * lanes + tap * channels
+            out_w_ref[:, start : start + channels] = raw_out_ref[tap // 3 * 9 + part * 3 + tap % 3]
+        out_w_ref[:, part * lanes + depth : (part + 1) * lanes] = jnp.zeros(
+            (out_w_ref.shape[0], lanes - depth), jnp.bfloat16
+        )
     for frame in range(frames):
         lay(rms_silu(features_ref[rows_of(frame), :].astype(jnp.float32), gain1), 2 + frame)
     advance(0, 0)
@@ -264,10 +273,12 @@
         halo_copy(0, frame).wait()
         lay(rms_silu(unpack(0, frame), gain1), frame)
     for step in range(1, half_way):
+        if step == 1:
+            begin(1)
         advance(0, step)
-        if step == half_way - 2:
-            begin(1)
-    if half_way < 3:
+        if step >= 2:
+            advance(1, step - 2)
+    if half_way < 2:
         begin(1)
     finish(0)
 
@@ -277,12 +288,12 @@
         value = rms_silu(first, gain2)
         pack(value.astype(jnp.float32), 1, frame)
         halo_copy(1, frame).start()
-        if frame < half_way:
-            advance(1, frame)
+        if max(0, half_way - 2) + frame < half_way:
+            advance(1, max(0, half_way - 2) + frame)
         own.append(value)
     for frame in range(frames):
         lay(own[frame], 2 + frame)
-    for step in range(frames, half_way):
+    for step in range(max(0, half_way - 2) + frames, half_way):
         advance(1, step)
     for frame in range(frames):
         halo_copy(1, frame).wait()
@@ -429,6 +440,7 @@
             dma((2, 1 + 6 * hops)), dma((2, 1 + 6 * hops)),
             dma((1,)), dma((3, frames)), dma((3, frames)),
             dma((chips,)), dma((chips,)), dma((chips,)), dma((chips,)),
+            pltpu.VMEM((latents, 3 * lanes), jnp.bfloat16),
         ],
         compiler_params=pltpu.CompilerParams(
             collective_id=0, has_side_effects=True, vmem_limit_bytes=60 * 1024 * 1024
@@ -439,7 +451,7 @@
         gain_first.reshape(1, channels), gain_second.reshape(1, channels),
         gain_third.reshape(1, channels),
         prepare(weight_first, lanes, whole_rows), prepare(weight_second, lanes, whole_rows),
-        prepare(weight_out, lanes, latents),
+        weight_out.transpose(0, 2, 1),
         jnp.asarray(place, jnp.bfloat16), token_order.reshape(1, count),
         jnp.asarray(pool, jnp.bfloat16), jnp.asarray(keep, jnp.bfloat16),
     )

time: 72.1 us -> 65.2 us (0.904)
  Pallas kernels: 67.2 us -> 61.5 us
  local copies, waits for them, and re-layouts: 4.57 us -> 3.31 us
    pallas_call x1, Pallas kernels: 62.9 us -> 57.3 us  [body(): pl.pallas_call(functools.partial(block_kernel, n, pairs, per, frames, hei...]
    unnamed x8 -> x4, local copies, waits for them, and re-layouts: 2.19 us -> 1.38 us
where the time goes in v3:
time: 65.2 us; the launch traced here: 64.9 us
  Pallas kernels  61.5 us (94%)
  local copies, waits for them, and re-layouts  3.31 us (5%)
    pallas_call x1, Pallas kernels, body(): pl.pallas_call(functools.partial(block_kernel, n, pairs, per, frames, hei...  57.3 us
    pallas_call x1, Pallas kernels, body(): pl.pallas_call(modulate_kernel, out_shape=jax.ShapeDtypeStruct((count, wi...  4.26 us
    unnamed x4, local copies, waits for them, and re-layouts  1.38 us

profile of v3, /device:TPU:0, one launch (start us, length us, event | category | flops | bytes accessed | tf_op | source)
XLA Modules:
  0.0 64.9 jit_solution(11499235440297129397)
XLA Ops:
  0.0 0.0 copy-start
  0.0 1.1 %reshape.43 = bf16[3,3,3,192,12]{3,2,1,0,4:T(4,128)(2,1)S(1)} reshape(bf16[27,192,12]{1,0,2:T(8,128)(2,1)} %param.18) | data formatting | bytes 248832 | tf_op jit(solution)/shard_map/reshape | solution.py:386
  1.1 0.1 copy.18
  1.2 0.2 reshape.44
  1.4 0.1 pad.7
  1.5 0.7 %copy.20 = bf16[2,8,3,1792]{3,1,2,0:T(8,128)(2,1)} copy(bf16[2,8,3,1792]{3,2,1,0:T(4,128)(2,1)S(1)} %bitcast.19) | data formatting | bytes 344064
  2.2 0.0 copy-done
  2.2 0.1 reshape.46
  2.3 0.1 copy.19
  2.4 0.2 reshape.47
  2.6 0.1 pad.8
  2.7 0.7 %copy.21 = bf16[2,8,3,1792]{3,1,2,0:T(8,128)(2,1)} copy(bf16[2,8,3,1792]{3,2,1,0:T(4,128)(2,1)S(1)} %bitcast.18) | data formatting | bytes 344064
  3.4 57.3 %block.1.ordered_ref = bf16[192,128]{1,0:T(8,128)(2,1)} custom-call(s32[32]{0:T(128)} %clip_ref.1, bf16[768,192]{1,0:T(8,128)(2,1)} %bitcast.24, f32[1,192]{1,0:T(1,128)} %bitcast.28, f32[1,192]{1,0:T(1,128)} %bitcast.29, f32[1,192]{1,0:T(1,128)} %bitcast.30, bf16[16,5376]{1,0:T(8,128)(2,1)} %bitcast.22, bf16[16,5376]{1,0:T(8,128)(2,1)} %bitcast.23, ...), custom_call_target="tpu_custom_call" | custom-call | tf_op jit(solution)/shard_map/block/pallas_call | solution.py:425
  60.6 4.3 %modulate.1 = bf16[192,3072]{1,0:T(8,128)(2,1)} custom-call(bf16[192,128]{1,0:T(8,128)(2,1)} %block.1.ordered_ref, bf16[64,3072]{1,0:T(8,128)(2,1)} %embed_ref.1, f32[1,3072]{1,0:T(1,128)} %bitcast.26, f32[1,3072]{1,0:T(1,128)} %bitcast.27), custom_call_target="tpu_custom_call" | custom-call | tf_op jit(solution)/shard_map/modulate/pallas_call | solution.py:459
Async XLA Ops:
  0.0 2.2 %copy-start = (bf16[27,192,12]{1,0,2:T(8,128)(2,1)S(1)}, bf16[27,192,12]{1,0,2:T(8,128)(2,1)}, u32[]{:S(2)}) copy-start(bf16[27,192,12]{1,0,2:T(8,128)(2,1)} %param.20) | copy-start | bytes 373252

commit v4 on v3

--- a/solution.py
+++ b/solution.py
@@ -38,7 +38,7 @@
     ordered_ref,
     gathered, halo, acts, taps, latent, patches, final,
     ring_send, ring_recv, cross_send, cross_recv, pair_send, pair_recv, local_sem,
-    halo_send, halo_recv, patch_send, patch_recv, fwd_send, fwd_recv, out_w_ref,
+    halo_send, halo_recv, patch_send, patch_recv, fwd_send, fwd_recv, out_w_ref, own_ref,
 ):
     me = lax.axis_index("ctx")
     group = lax.axis_index("groups")
@@ -79,9 +79,15 @@
             gathered[w, me, part, :, lanes:] = rest.astype(jnp.bfloat16)
         gathered[w, me, part, :, :lanes] = values[:rows]
 
-    for part in range(3):
-        for w, own in enumerate((own1_ref, own2_ref)):
-            place_own(w, part, own[:, part * lanes : (part + 1) * lanes])
+    def lay_own(w, raw):
+        own_ref[w] = jnp.zeros(own_ref.shape[1:], jnp.bfloat16)
+        for part in range(3):
+            for tap in range(9):
+                start = part * lanes + tap * channels
+                own_ref[w, :per, start : start + channels] = raw[:, tap // 3 * 9 + part * 3 + tap % 3, :]
+            place_own(w, part, own_ref[w, :, part * lanes : (part + 1) * lanes])
+
+    lay_own(0, own1_ref)
     for frame in range(frames):
         pack(features_ref[rows_of(frame), :].astype(jnp.float32), 0, frame)
 
@@ -259,6 +265,7 @@
 
     gain1, gain2, gain3 = gain1_ref[...], gain2_ref[...], gain3_ref[...]
 
+    lay_own(1, own2_ref)
     for part in range(3):
         for tap in range(9):
             start = part * lanes + tap * channels
@@ -370,9 +377,9 @@
 
 
 def modulate_kernel(ordered_ref, embed_ref, shift_ref, scale_ref, out_ref):
-    embed = embed_ref[...]
-    both = jnp.concatenate([embed, embed], axis=0)
-    embedded = jnp.dot(ordered_ref[...], both, preferred_element_type=jnp.float32)
+    half = embed_ref.shape[0]
+    ordered = ordered_ref[:, :half] + ordered_ref[:, half:]
+    embedded = jnp.dot(ordered, embed_ref[...], preferred_element_type=jnp.float32)
     inverse = 1.0 / embedded.shape[1]
     center = jnp.sum(embedded, axis=-1, keepdims=True) * inverse
     centered = embedded - center
@@ -441,6 +448,7 @@
             dma((1,)), dma((3, frames)), dma((3, frames)),
             dma((chips,)), dma((chips,)), dma((chips,)), dma((chips,)),
             pltpu.VMEM((latents, 3 * lanes), jnp.bfloat16),
+            pltpu.VMEM((2, whole_rows, 3 * lanes), jnp.bfloat16),
         ],
         compiler_params=pltpu.CompilerParams(
             collective_id=0, has_side_effects=True, vmem_limit_bytes=60 * 1024 * 1024
@@ -450,7 +458,7 @@
         clip_ids, features.reshape(frames * size, channels),
         gain_first.reshape(1, channels), gain_second.reshape(1, channels),
         gain_third.reshape(1, channels),
-        prepare(weight_first, lanes, whole_rows), prepare(weight_second, lanes, whole_rows),
+        weight_first.transpose(2, 0, 1), weight_second.transpose(2, 0, 1),
         weight_out.transpose(0, 2, 1),
         jnp.asarray(place, jnp.bfloat16), token_order.reshape(1, count),
         jnp.asarray(pool, jnp.bfloat16), jnp.asarray(keep, jnp.bfloat16),

time: 65.2 us -> 62.2 us (0.954)
  local copies, waits for them, and re-layouts: 3.31 us -> 0 us
    reshape x4 -> x0, local copies, waits for them, and re-layouts: 1.61 us -> none  [the longest x2 1.18 us: prepare(): split = weight.reshape(3, 3, 3, channels, outs).transpose(4, 1, 0, 2, 3)]
    unnamed x4 -> x0, local copies, waits for them, and re-layouts: 1.38 us -> none
where the time goes in v4:
time: 62.2 us; the launch traced here: 61.9 us
  Pallas kernels  61.9 us (100%)
    pallas_call x1, Pallas kernels, body(): pl.pallas_call(functools.partial(block_kernel, n, pairs, per, frames, hei...  57.5 us
    pallas_call x1, Pallas kernels, body(): pl.pallas_call(modulate_kernel, out_shape=jax.ShapeDtypeStruct((count, wi...  4.33 us

profile of v4, /device:TPU:0, one launch (start us, length us, event | category | flops | bytes accessed | tf_op | source)
XLA Modules:
  0.0 61.9 jit_solution(16539788599821859386)
XLA Ops:
  0.0 57.5 %block.1.ordered_ref = bf16[192,128]{1,0:T(8,128)(2,1)} custom-call(s32[32]{0:T(128)} %clip_ref.1, bf16[768,192]{1,0:T(8,128)(2,1)} %bitcast.10, f32[1,192]{1,0:T(1,128)} %bitcast.16, f32[1,192]{1,0:T(1,128)} %bitcast.17, f32[1,192]{1,0:T(1,128)} %bitcast.18, bf16[12,27,192]{2,1,0:T(8,128)(2,1)} %bitcast.12, bf16[12,27,192]{2,1,0:T(8,128)(2,1)} %bitcast.13, ...), custom_call_target="tpu_custom_call" | custom-call | tf_op jit(solution)/shard_map/block/pallas_call | solution.py:432
  57.5 4.3 %modulate.1 = bf16[192,3072]{1,0:T(8,128)(2,1)} custom-call(bf16[192,128]{1,0:T(8,128)(2,1)} %block.1.ordered_ref, bf16[64,3072]{1,0:T(8,128)(2,1)} %embed_ref.1, f32[1,3072]{1,0:T(1,128)} %bitcast.14, f32[1,3072]{1,0:T(1,128)} %bitcast.15), custom_call_target="tpu_custom_call" | custom-call | tf_op jit(solution)/shard_map/modulate/pallas_call | solution.py:467
